TPU v7x, 512 devices: a whole 4x8x8 slice. The times are simulated.
512 devices in a mesh: dp: 32 (over z_lo, y, core), blk: 16 (over z_hi, x).
Axes of the slice: x: 4, y: 8, z: 8 (z_hi: 4, z_lo: 2; z = z_hi * 2 + z_lo), core: 2. Of those that a mesh axis runs over, the one named last changes fastest.
Arguments:
- hidden_in: bfloat16 [12288, 1152], P(('dp', 'blk')), may hold values from -6 to 6
- gain_mlp: float32 [1152], replicated, may hold values from 0.1 to 1.9
- gain_final: float32 [1152], replicated, may hold values from 0.1 to 1.9
- w_in: bfloat16 [1152, 4304], P(None, 'blk'), may hold values from -0.1875 to 0.1875
- w_out: bfloat16 [4304, 1152], P('blk'), may hold values from -0.09375 to 0.09375
- image_embeds: bfloat16 [12288, 1152], P(('dp', 'blk')), may hold values from -6 to 6
- pair_ids: int32 [12288], P(('dp', 'blk')), may hold values from 0 to 383
- teacher_logits: bfloat16 [32, 384, 384], P('dp', None, 'blk'), may hold values from -12 to 12
Outputs:
- grad_hidden: float32 [12288, 1152], P(('dp', 'blk'))
- grad_w_in: float32 [1152, 4304], P(None, 'blk')
- grad_w_out: float32 [4304, 1152], P('blk')
All inputs are finite; a program needn't handle non-finite values.
Results may differ from a plain program's by a relative error of at most 0.0067.
Values may be sent and summed in bfloat16 or wider, within the bound.
No kernel may reach another device: no remote copies, remote signals or barrier semaphores. Data moves between devices by JAX's collectives and lax.ppermute only.
A program may use at most 64 MiB of HBM per device.

v0:
```python
import jax
import jax.numpy as jnp
from jax import lax
from jax.experimental import pallas as pl
from jax.experimental.pallas import tpu as pltpu
from jax.sharding import Mesh
from jax.sharding import PartitionSpec as P


epsilon = 1e-06
logit_scale = 10.0
logit_bias = -2.0
gelu_coeff = 0.7978845608028654

DP = ("zl", "y", "co")
BLK = ("zh", "x")
ARRIVAL = ("x", "zh")
RING = ("zl", "y")
LANES = 128
VMEM_GRANT = 8 * 2**20
WHOLE_GRANT = 60 * 2**20
F32 = jnp.float32
BF16 = jnp.bfloat16

NT = (((1,), (1,)), ((), ()))
TN = (((0,), (0,)), ((), ()))
NN = (((1,), (0,)), ((), ()))


def shape(dims, dtype):
    return jax.ShapeDtypeStruct(dims, dtype)


def call(body, outs, *args, far_in=(), scratch=(), flops=0, grant=VMEM_GRANT):
    size = sum(a.size * a.dtype.itemsize for a in args)
    size += sum(o.size * o.dtype.itemsize for o in outs)
    near = pl.BlockSpec(memory_space=pltpu.VMEM)
    far = pl.BlockSpec(memory_space=pl.ANY)
    return pl.pallas_call(
        body,
        out_shape=tuple(outs),
        in_specs=[far if k in far_in else near for k in range(len(args))],
        out_specs=tuple([near] * len(outs)),
        scratch_shapes=list(scratch),
        compiler_params=pltpu.CompilerParams(vmem_limit_bytes=grant),
        cost_estimate=pl.CostEstimate(flops=flops, bytes_accessed=size, transcendentals=0),
    )(*args)


def dot(a, b, dims):
    return lax.dot_general(a, b, dims, preferred_element_type=F32)


def norm_parts(values):
    row_mean = jnp.mean(values, axis=-1, keepdims=True)
    centred = values - row_mean
    variance = jnp.mean(centred * centred, axis=-1, keepdims=True)
    inverse = lax.rsqrt(variance + epsilon)
    return centred * inverse, inverse


def norm_backward(grad_normed, normed, inverse):
    mean_grad = jnp.mean(grad_normed, axis=-1, keepdims=True)
    mean_cross = jnp.mean(grad_normed * normed, axis=-1, keepdims=True)
    return inverse * (grad_normed - mean_grad - normed * mean_cross)


def gelu_both(pre_act):
    inner_arg = gelu_coeff * (pre_act + 0.044715 * pre_act * pre_act * pre_act)
    tangent = jnp.tanh(inner_arg)
    gelu_value = 0.5 * pre_act * (1.0 + tangent)
    gelu_slope = 0.5 * (1.0 + tangent) + 0.5 * pre_act * (1.0 - tangent * tangent) * gelu_coeff * (
        1.0 + 3.0 * 0.044715 * pre_act * pre_act
    )
    return gelu_value, gelu_slope


def column_of(row_ref):
    count = row_ref.shape[1]
    spread = jnp.broadcast_to(row_ref[...], (count, count))
    down = lax.broadcasted_iota(jnp.int32, (count, count), 0)
    along = lax.broadcasted_iota(jnp.int32, (count, count), 1)
    return jnp.sum(jnp.where(down == along, spread, 0), axis=1, keepdims=True)


def prepare(
    hidden_hbm, gain_hbm, image_hbm, id_hbm, out_ref, hidden_ref, gain_ref, image_ref, id_ref, sems
):
    width = hidden_ref.shape[1]
    arrays = ((hidden_hbm, hidden_ref), (gain_hbm, gain_ref), (image_hbm, image_ref), (id_hbm, id_ref))
    moves = [pltpu.make_async_copy(src, dst, sems.at[k]) for k, (src, dst) in enumerate(arrays)]
    for move in moves:
        move.start()
    for move in moves:
        move.wait()
    normed, _ = norm_parts(hidden_ref[...].astype(F32))
    out_ref[:, :width] = (normed * gain_ref[...].reshape(1, width)).astype(BF16)
    image = image_ref[...].astype(F32)
    scale = lax.rsqrt(jnp.sum(image * image, axis=-1, keepdims=True) + epsilon)
    out_ref[:, width : 2 * width] = (image * scale).astype(BF16)
    ids = column_of(id_ref)
    lane = lax.broadcasted_iota(jnp.int32, (image.shape[0], LANES), 1)
    low = jnp.where(lane == 0, ids & 127, 0)
    high = jnp.where(lane == 1, ids >> 7, 0)
    out_ref[:, 2 * width :] = (low + high).astype(F32).astype(BF16)


def split(both_ref, rows_ref, image_ref):
    width = rows_ref.shape[2]
    rows_ref[...] = both_ref[:, :, :width]
    image_ref[...] = both_ref[:, :, width:]


def targets(image_ref, teacher_ref, id_ref, target_ref):
    sides, _, rows, deep = image_ref.shape
    group = sides * sides * rows
    marks = image_ref[:, :, :, deep - LANES :].reshape(group, LANES)
    row = lax.broadcasted_iota(jnp.int32, (8, LANES), 0)
    lane = lax.broadcasted_iota(jnp.int32, (8, LANES), 1)
    pick = jnp.where(row == lane, 1.0, 0.0).astype(BF16)
    ids = dot(pick, marks, NT)
    image_id = ids[0:1] + 128.0 * ids[1:2]
    text_id = column_of(id_ref).astype(F32)
    same = jnp.where(text_id == image_id, 0.5, 0.0)
    down = lax.broadcasted_iota(jnp.int32, (group, group), 0)
    along = lax.broadcasted_iota(jnp.int32, (1, group), 1)
    block = along // rows
    wanted = (lax.rem(block, sides) * sides + block // sides) * rows + lax.rem(along, rows)
    order = jnp.where(down == wanted, 1.0, 0.0).astype(BF16)
    teacher = dot(teacher_ref[...], order, NN)
    target_ref[...] = same + 0.5 * jax.nn.sigmoid(teacher)


def forward(all_ref, w_in_ref, w_out_ref, part_ref):
    blocks, rows, width = part_ref.shape
    pre_act = dot(all_ref[...].reshape(blocks * rows, width), w_in_ref[...], NT)
    value, _ = gelu_both(pre_act)
    part = dot(value.astype(BF16), w_out_ref[...], NN).astype(BF16)
    part_ref[...] = part.reshape(blocks, rows, width)


def middle(part_ref, hidden_ref, gain_ref, image_ref, target_ref, out_ref, grad_ref):
    blocks, rows, width = part_ref.shape
    total = part_ref[0].astype(F32)
    for k in range(1, blocks):
        total = total + part_ref[k].astype(F32)
    residual = hidden_ref[...].astype(F32) + total
    gain = gain_ref[...].reshape(1, width)
    normed, inverse = norm_parts(residual)
    final = normed * gain
    length = jnp.sqrt(jnp.sum(final * final, axis=-1, keepdims=True) + epsilon)
    unit = final / length
    images = image_ref[:, :, :, :width].reshape(blocks * rows, width)
    logits = dot(unit.astype(BF16), images, NT) * logit_scale + logit_bias
    pair_grad = (jax.nn.sigmoid(logits) - target_ref[...]).astype(BF16)
    text_grad = logit_scale * dot(pair_grad, images, NN)
    radial = jnp.sum(unit * text_grad, axis=-1, keepdims=True)
    grad_final = (text_grad - unit * radial) / length
    grad = norm_backward(grad_final * gain, normed, inverse)
    grad_ref[...] = grad
    sent = grad.astype(BF16)
    for k in range(blocks):
        out_ref[k] = sent


def backward(all_ref, w_in_ref, rows_ref, w_out_ref, grad_ref, act_ref):
    blocks, rows, width = rows_ref.shape
    group = blocks * rows
    pre_act = dot(all_ref[...].reshape(group, width), w_in_ref[...], NT)
    value, slope = gelu_both(pre_act)
    act_ref[...] = value.astype(BF16)
    grad_act = dot(rows_ref[...].reshape(group, width), w_out_ref[...], NT)
    grad_ref[...] = (grad_act * slope).astype(BF16)


def input_grad(grad_ref, w_in_ref, k0, k1, k2, k3, held):
    at = lax.axis_index("x")
    held[...] = dot(grad_ref[...], w_in_ref[...], NN).astype(BF16).reshape(held.shape)
    for k, out in enumerate((k0, k1, k2, k3)):
        x = lax.rem(at + k, 4)
        for z in range(4):
            out[z] = held[x * 4 + z]


def packed(a_ref, b_ref, out_ref):
    a = a_ref[...]
    units = a.shape[1]
    width = b_ref.shape[-1]
    blocks = width // LANES
    even = units // 8 * 8
    odd = units - even
    full = dot(a, b_ref[...].reshape(a.shape[0], width), TN).astype(out_ref.dtype)
    for c in range(blocks):
        tile = full[:, c * LANES : (c + 1) * LANES]
        out_ref[c * even : (c + 1) * even, :] = tile[:even]
        if odd:
            out_ref[blocks * even + c * odd : blocks * even + (c + 1) * odd, :] = tile[even:]


def weight_grad(first, act_ref, grads_ref, pre_ref, rows_ref, out_ref):
    units = act_ref.shape[1]
    width = grads_ref.shape[-1]
    core = lax.axis_index("co")
    used = units * (width // LANES) // 8 * 8
    tall = out_ref.shape[0]
    if used < tall:
        out_ref[used:tall, :] = jnp.zeros((tall - used, LANES), out_ref.dtype)

    @pl.when(core == first)
    def _():
        packed(act_ref, grads_ref, out_ref)

    @pl.when(core != first)
    def _():
        packed(pre_ref, rows_ref, out_ref)


def join(kept_ref, got_ref, out_ref):
    ring, chunk, lanes = out_ref.shape
    total = kept_ref[...] + got_ref[...].astype(F32)
    out_ref[...] = total.astype(BF16).reshape(ring, chunk, lanes)


def ring_sum(slices_ref, out_ref):
    total = slices_ref[0].astype(F32)
    for k in range(1, slices_ref.shape[0]):
        total = total + slices_ref[k].astype(F32)
    sent = total.astype(BF16)
    for k in range(out_ref.shape[0]):
        out_ref[k] = sent


def unpack(mine_ref, other_ref, w_out_ref, w_in_ref):
    units, width = w_out_ref.shape
    core = lax.axis_index("co")
    blocks = width // LANES
    even = units // 8 * 8
    odd = units - even

    def spread(src, dst):
        for c in range(blocks):
            lanes = slice(c * LANES, (c + 1) * LANES)
            dst[:even, lanes] = src[c * even : (c + 1) * even, :].astype(F32)
            if odd:
                at = blocks * even + c * odd
                dst[even:, lanes] = src[at : at + odd, :].astype(F32)

    @pl.when(core == 0)
    def _():
        spread(mine_ref, w_out_ref)
        spread(other_ref, w_in_ref)

    @pl.when(core != 0)
    def _():
        spread(other_ref, w_out_ref)
        spread(mine_ref, w_in_ref)


def column_sum(k0, k1, k2, k3, keep_ref, s1, s2, s3, held):
    at = lax.axis_index("zh")
    total = k0[...].astype(F32) + k1[...].astype(F32)
    held[...] = total + k2[...].astype(F32) + k3[...].astype(F32)
    keep_ref[...] = held[at]
    for k, out in enumerate((s1, s2, s3)):
        out[...] = held[lax.rem(at + k + 1, 4)].astype(BF16)


def last(keep_ref, g1, g2, g3, hidden_ref, gain_ref, grad_ref, out_ref):
    total = keep_ref[...] + g1[...].astype(F32) + g2[...].astype(F32) + g3[...].astype(F32)
    normed, inverse = norm_parts(hidden_ref[...].astype(F32))
    out_ref[...] = grad_ref[...] + norm_backward(total * gain_ref[...].reshape(1, -1), normed, inverse)


def shift(value, axis, by):
    length = lax.axis_size(axis)
    return lax.ppermute(value, axis, [(i, (i + by) % length) for i in range(length)])


def per_device(
    hidden_in, gain_mlp, gain_final, w_in, w_out, image_embeds, pair_ids, teacher_logits
):
    rows, width = hidden_in.shape
    units = w_in.shape[1]
    blocks = lax.axis_size(BLK)
    ring = lax.axis_size(RING)
    group = rows * blocks
    ids = pair_ids.reshape(1, rows)
    w_in_rows = w_in.T
    teacher = teacher_logits[0].T
    spread = shape((blocks, rows, width), BF16)
    matmul = 2 * group * units * width

    (own_rows,) = call(
        prepare,
        [shape((rows, 2 * width + LANES), BF16)],
        hidden_in,
        gain_mlp,
        image_embeds,
        ids,
        far_in=(0, 1, 2, 3),
        scratch=[
            pltpu.VMEM(hidden_in.shape, BF16),
            pltpu.VMEM(gain_mlp.shape, F32),
            pltpu.VMEM(image_embeds.shape, BF16),
            pltpu.VMEM(ids.shape, ids.dtype),
            pltpu.SemaphoreType.DMA((4,)),
        ],
        grant=WHOLE_GRANT,
    )
    both = lax.all_gather(own_rows, "zh")
    rows_column, column = call(
        split, [shape((4, rows, width), BF16), shape((4, rows, width + LANES), BF16)], both
    )
    group_input = lax.all_gather(rows_column, "x")
    (part,) = call(forward, [spread], group_input, w_in_rows, w_out, flops=2 * matmul)
    part, column = lax.optimization_barrier((part, column))
    images = lax.all_gather(column, "x")
    (target,) = call(targets, [shape((rows, group), F32)], images, teacher, ids)
    parts = lax.all_to_all(part, ARRIVAL, 0, 0)
    copies, grad_residual = call(
        middle, [spread, shape((rows, width), F32)], parts, hidden_in, gain_final, images, target
    )
    group_grads = lax.all_to_all(copies, ARRIVAL, 0, 0)
    grad_pre, act = call(
        backward,
        [shape((group, units), BF16)] * 2,
        group_input,
        w_in_rows,
        group_grads,
        w_out,
        flops=2 * matmul,
    )

    chunk = -(-(units * (width // LANES)) // (8 * ring)) * 8
    tall = chunk * ring

    def grads(first, dtype):
        return call(
            lambda *refs: weight_grad(first, *refs),
            [shape((tall, LANES), dtype)],
            act,
            group_grads,
            grad_pre,
            group_input,
            flops=matmul,
        )[0]

    give = grads(1, BF16)
    got = shift(give, "co", 1)
    keep = grads(0, F32)
    (mine,) = call(join, [shape((ring, chunk, LANES), BF16)], keep, got)
    slices = lax.all_to_all(mine, RING, 0, 0)

    quarter = shape((4, rows, width), BF16)
    k0, s1, s2, s3 = call(
        input_grad,
        [quarter] * 4,
        grad_pre,
        w_in_rows,
        flops=matmul,
        scratch=[pltpu.VMEM((blocks, rows, width), BF16)],
    )
    arrived = []
    for k, sent in ((1, s1), (2, s2), (3, s3)):
        arrived.append(shift(sent, "x", k))
    own, s1, s2, s3 = call(
        column_sum,
        [shape((rows, width), F32)] + [shape((rows, width), BF16)] * 3,
        k0,
        *arrived,
        scratch=[pltpu.VMEM((4, rows, width), F32)],
    )
    arrived = []
    for k, sent in ((1, s1), (2, s2), (3, s3)):
        arrived.append(shift(sent, "zh", k))
    (grad_hidden,) = call(
        last, [shape((rows, width), F32)], own, *arrived, hidden_in, gain_mlp, grad_residual
    )

    (copies,) = call(ring_sum, [shape((ring, chunk, LANES), BF16)], slices)
    whole = lax.all_to_all(copies, RING, 0, 0).reshape(tall, LANES)
    other = shift(whole, "co", 1)
    grad_w_out, grad_w_in = call(unpack, [shape((units, width), F32)] * 2, whole, other)
    return (grad_hidden, grad_w_in.T, grad_w_out)


def solution(mesh):
    fine = Mesh(mesh.devices.reshape(2, 8, 2, 4, 4), ("zl", "y", "co", "zh", "x"))
    every = DP + BLK
    in_specs = (
        P(every, None),
        P(),
        P(),
        P(None, BLK),
        P(BLK, None),
        P(every, None),
        P(every),
        P(DP, None, BLK),
    )
    out_specs = (P(every, None), P(None, BLK), P(BLK, None))
    return jax.shard_map(
        per_device, mesh=fine, in_specs=in_specs, out_specs=out_specs, check_vma=False
    )
```

profile of v0, /device:TPU:1, one launch (start us, length us, event | category | flops | bytes accessed | tf_op | source)
XLA Modules:
  0.0 193.6 jit_solution(11912025107919657420)
XLA Ops:
  0.7 1.8 shard_map.103
  2.5 20.2 %all-gather = bf16[96,2432]{1,0:T(8,128)(2,1)S(1)} all-gather(bf16[24,2432]{1,0:T(8,128)(2,1)} %shard_map.103), channel_id=2, replica_groups=mesh['zl'=2,'y'=8,'co'=2,'zh'=4,'x'=4] {'zh'}, dimensions={0}, use_global_device_ids=true | all-gather | bytes 583680 | tf_op jit(solution)/shard_map/all_gather | solution.py:310
  22.7 0.7 copy-done.4
  23.4 11.7 %all-gather.1 = bf16[16,24,1152]{2,1,0:T(8,128)(2,1)S(1)} all-gather(bf16[4,24,1152]{2,1,0:T(8,128)(2,1)S(1)} %get-tuple-element.21), channel_id=3, replica_groups=mesh['zl'=2,'y'=8,'co'=2,'zh'=4,'x'=4] {'x'}, dimensions={0}, use_global_device_ids=true | all-gather | bytes 1105920 | tf_op jit(solution)/shard_map/all_gather | solution.py:314
  35.2 2.2 %shard_map.105 = bf16[16,24,1152]{2,1,0:T(8,128)(2,1)} custom-call(bf16[4,4,24,1152]{3,2,1,0:T(8,128)(2,1)S(1)} %bitcast.10, bf16[269,1152]{1,0:T(8,128)(2,1)S(1)} %bitcast.16, bf16[269,1152]{1,0:T(8,128)(2,1)S(1)} %copy-done.1), custom_call_target="tpu_custom_call" | custom-call | flops 475987968 | bytes 3009024 | tf_op jit(solution)/shard_map/pallas_call | solution.py:39
  37.4 6.6 %all-to-all-start = ((bf16[16,24,1152]{2,1,0:T(8,128)(2,1)}), bf16[16,24,1152]{2,1,0:T(8,128)(2,1)S(1)}, u32[]{:S(2)}, u32[]{:S(2)}) async-start(bf16[16,24,1152]{2,1,0:T(8,128)(2,1)} %shard_map.105), calls=%async_computation | async-start | bytes 1769472 | tf_op jit(solution)/shard_map/all_to_all | solution.py:319
  44.1 17.8 %all-gather.2 = bf16[16,24,1280]{2,1,0:T(8,128)(2,1)S(1)} all-gather(bf16[4,24,1280]{2,1,0:T(8,128)(2,1)} %copy-done.4), channel_id=4, replica_groups=mesh['zl'=2,'y'=8,'co'=2,'zh'=4,'x'=4] {'x'}, dimensions={0}, use_global_device_ids=true | all-gather | bytes 1228800 | tf_op jit(solution)/shard_map/all_gather | solution.py:317
  61.9 0.2 shard_map.106.target_ref
  62.1 1.3 shard_map.107
  63.4 25.3 %all_to_all.20.rows_ref.refs_1_ = bf16[16,24,1152]{2,1,0:T(8,128)(2,1)S(1)} all-to-all(bf16[16,24,1152]{2,1,0:T(8,128)(2,1)S(1)} %get-tuple-element.25), channel_id=1, replica_groups=mesh['zl'=2,'y'=8,'co'=2,'zh'=4,'x'=4] {'x','zh'}, dimensions={0} | all-to-all | bytes 1769472 | tf_op jit(solution)/shard_map/all_to_all | solution.py:323
  88.7 1.2 shard_map.108
  89.9 0.6 shard_map.113
  90.5 12.8 %collective-permute-start.6 = (bf16[2432,128]{1,0:T(8,128)(2,1)S(1)}, bf16[2432,128]{1,0:T(8,128)(2,1)S(1)}, u32[]{:S(2)}, u32[]{:S(2)}) collective-permute-start(bf16[2432,128]{1,0:T(8,128)(2,1)S(1)} %shard_map.113), channel_id=1, source_target_pairs={{0,16},{16,0},{1,17},{17,1},{2,18},{18,2},{3,19},{19,3},{4,20},{20... | collective-permute-start | bytes 1867784 | tf_op jit(solution)/shard_map/ppermute | solution.py:276
  103.3 0.6 shard_map.112.kept_ref
  103.9 1.1 collective-permute-done.6.got_ref
  105.1 24.3 %all_to_all.21.slices_ref = bf16[16,152,128]{2,1,0:T(8,128)(2,1)S(1)} all-to-all(bf16[16,152,128]{2,1,0:T(8,128)(2,1)S(1)} %shard_map.114), channel_id=1, replica_groups=mesh['zl'=2,'y'=8,'co'=2,'zh'=4,'x'=4] {'zl','y'}, dimensions={0} | all-to-all | bytes 1245184 | tf_op jit(solution)/shard_map/all_to_all | solution.py:352
  129.5 22.2 %all_to_all.22 = bf16[16,152,128]{2,1,0:T(8,128)(2,1)S(1)} all-to-all(bf16[16,152,128]{2,1,0:T(8,128)(2,1)S(1)} %shard_map.115), channel_id=1, replica_groups=mesh['zl'=2,'y'=8,'co'=2,'zh'=4,'x'=4] {'zl','y'}, dimensions={0} | all-to-all | bytes 1245184 | tf_op jit(solution)/shard_map/all_to_all | solution.py:381
  151.7 5.0 %collective-permute-start.7 = (bf16[2432,128]{1,0:T(8,128)(2,1)S(1)}, bf16[2432,128]{1,0:T(8,128)(2,1)S(1)}, u32[]{:S(2)}, u32[]{:S(2)}) collective-permute-start(bf16[2432,128]{1,0:T(8,128)(2,1)S(1)} %bitcast.19), channel_id=1, source_target_pairs={{0,16},{16,0},{1,17},{17,1},{2,18},{18,2},{3,19},{19,3},{4,20},{20... | collective-permute-start | bytes 1867784 | tf_op jit(solution)/shard_map/ppermute | solution.py:276
  156.6 0.7 shard_map.109
  157.4 3.3 %collective-permute-start = (bf16[4,24,1152]{2,1,0:T(8,128)(2,1)S(1)}, bf16[4,24,1152]{2,1,0:T(8,128)(2,1)S(1)}, u32[]{:S(2)}, u32[]{:S(2)}) collective-permute-start(bf16[4,24,1152]{2,1,0:T(8,128)(2,1)S(1)} %get-tuple-element.28), channel_id=1, source_target_pairs={{0,1},{1,2},{2,3},{3,0},{4,5},{5,6},{6,7},{7,4},{8,9},{9,10},{10,1... | collective-permute-start | bytes 663560 | tf_op jit(solution)/shard_map/ppermute | solution.py:276
  160.7 2.3 %collective-permute-start.1 = (bf16[4,24,1152]{2,1,0:T(8,128)(2,1)S(1)}, bf16[4,24,1152]{2,1,0:T(8,128)(2,1)S(1)}, u32[]{:S(2)}, u32[]{:S(2)}) collective-permute-start(bf16[4,24,1152]{2,1,0:T(8,128)(2,1)S(1)} %get-tuple-element.29), channel_id=1, source_target_pairs={{0,2},{1,3},{2,0},{3,1},{4,6},{5,7},{6,4},{7,5},{8,10},{9,11},{10,... | collective-permute-start | bytes 663560 | tf_op jit(solution)/shard_map/ppermute | solution.py:276
  163.0 4.0 %collective-permute-start.2 = (bf16[4,24,1152]{2,1,0:T(8,128)(2,1)S(1)}, bf16[4,24,1152]{2,1,0:T(8,128)(2,1)S(1)}, u32[]{:S(2)}, u32[]{:S(2)}) collective-permute-start(bf16[4,24,1152]{2,1,0:T(8,128)(2,1)S(1)} %get-tuple-element.30), channel_id=1, source_target_pairs={{0,3},{1,0},{2,1},{3,2},{4,7},{5,4},{6,5},{7,6},{8,11},{9,8},{10,9... | collective-permute-start | bytes 663560 | tf_op jit(solution)/shard_map/ppermute | solution.py:276
  166.9 5.2 %collective-permute-done.k1 = bf16[4,24,1152]{2,1,0:T(8,128)(2,1)S(1)} collective-permute-done((bf16[4,24,1152]{2,1,0:T(8,128)(2,1)S(1)}, bf16[4,24,1152]{2,1,0:T(8,128)(2,1)S(1)}, u32[]{:S(2)}, u32[]{:S(2)}) %collective-permute-start) | collective-permute-done | bytes 221216 | tf_op jit(solution)/shard_map/ppermute | solution.py:276
  172.2 2.2 %collective-permute-done.2.k3 = bf16[4,24,1152]{2,1,0:T(8,128)(2,1)S(1)} collective-permute-done((bf16[4,24,1152]{2,1,0:T(8,128)(2,1)S(1)}, bf16[4,24,1152]{2,1,0:T(8,128)(2,1)S(1)}, u32[]{:S(2)}, u32[]{:S(2)}) %collective-permute-start.2) | collective-permute-done | bytes 221216 | tf_op jit(solution)/shard_map/ppermute | solution.py:276
  174.4 0.2 shard_map.110
  174.6 4.4 %collective-permute-start.3 = (bf16[24,1152]{1,0:T(8,128)(2,1)S(1)}, bf16[24,1152]{1,0:T(8,128)(2,1)S(1)}, u32[]{:S(2)}, u32[]{:S(2)}) collective-permute-start(bf16[24,1152]{1,0:T(8,128)(2,1)S(1)} %get-tuple-element.32), channel_id=1, source_target_pairs={{0,4},{4,8},{8,12},{12,0},{1,5},{5,9},{9,13},{13,1},{2,6},{6,10},{... | collective-permute-start | bytes 165896 | tf_op jit(solution)/shard_map/ppermute | solution.py:276
  179.0 2.4 %collective-permute-start.4 = (bf16[24,1152]{1,0:T(8,128)(2,1)S(1)}, bf16[24,1152]{1,0:T(8,128)(2,1)S(1)}, u32[]{:S(2)}, u32[]{:S(2)}) collective-permute-start(bf16[24,1152]{1,0:T(8,128)(2,1)S(1)} %get-tuple-element.33), channel_id=1, source_target_pairs={{0,8},{4,12},{8,0},{12,4},{1,9},{5,13},{9,1},{13,5},{2,10},{6,14},... | collective-permute-start | bytes 165896 | tf_op jit(solution)/shard_map/ppermute | solution.py:276
  181.4 5.0 %collective-permute-start.5 = (bf16[24,1152]{1,0:T(8,128)(2,1)S(1)}, bf16[24,1152]{1,0:T(8,128)(2,1)S(1)}, u32[]{:S(2)}, u32[]{:S(2)}) collective-permute-start(bf16[24,1152]{1,0:T(8,128)(2,1)S(1)} %get-tuple-element.34), channel_id=1, source_target_pairs={{0,12},{4,0},{8,4},{12,8},{1,13},{5,1},{9,5},{13,9},{2,14},{6,2},{... | collective-permute-start | bytes 165896 | tf_op jit(solution)/shard_map/ppermute | solution.py:276
  186.5 1.3 collective-permute-done.4.g2
  187.8 3.2 %collective-permute-done.5.g3 = bf16[24,1152]{1,0:T(8,128)(2,1)S(1)} collective-permute-done((bf16[24,1152]{1,0:T(8,128)(2,1)S(1)}, bf16[24,1152]{1,0:T(8,128)(2,1)S(1)}, u32[]{:S(2)}, u32[]{:S(2)}) %collective-permute-start.5) | collective-permute-done | bytes 55328 | tf_op jit(solution)/shard_map/ppermute | solution.py:276
  191.1 0.9 shard_map.111
  192.0 1.6 shard_map.116
  (24 shorter events, 0.3 us)
Async XLA Ops:
  0.6 34.5 %copy-start.1 = (bf16[269,1152]{1,0:T(8,128)(2,1)S(1)}, bf16[269,1152]{1,0:T(8,128)(2,1)}, u32[]{:S(2)}) copy-start(bf16[269,1152]{1,0:T(8,128)(2,1)} %w_out_ref.3) | copy-start | bytes 1859332
  0.6 34.5 %copy-start = (bf16[1152,269]{0,1:T(8,128)(2,1)S(1)}, bf16[1152,269]{0,1:T(8,128)(2,1)}, u32[]{:S(2)}) copy-start(bf16[1152,269]{0,1:T(8,128)(2,1)} %param.11) | copy-start | bytes 1859332
  22.7 0.7 copy-start.4
  37.4 24.5 %copy-start.6 = (bf16[1,384,24]{1,2,0:T(8,128)(2,1)S(1)}, bf16[1,384,24]{1,2,0:T(8,128)(2,1)}, u32[]{:S(2)}) copy-start(bf16[1,384,24]{1,2,0:T(8,128)(2,1)} %param.15) | copy-start | bytes 55300
  37.4 24.5 %copy-start.8 = (s32[24]{0:T(128)S(1)}, s32[24]{0:T(128)}, u32[]{:S(2)}) copy-start(s32[24]{0:T(128)} %param.14) | copy-start | bytes 292
  37.4 24.7 %all-to-all-start = ((bf16[16,24,1152]{2,1,0:T(8,128)(2,1)}), bf16[16,24,1152]{2,1,0:T(8,128)(2,1)S(1)}, u32[]{:S(2)}, u32[]{:S(2)}) async-start(bf16[16,24,1152]{2,1,0:T(8,128)(2,1)} %shard_map.105), calls=%async_computation | async-start | bytes 1769472 | tf_op jit(solution)/shard_map/all_to_all | solution.py:319
  44.1 18.1 %copy-start.3 = (bf16[24,1152]{1,0:T(8,128)(2,1)S(1)}, bf16[24,1152]{1,0:T(8,128)(2,1)}, u32[]{:S(2)}) copy-start(bf16[24,1152]{1,0:T(8,128)(2,1)} %hidden_ref.3) | copy-start | bytes 165892
  44.1 18.1 %copy-start.7 = (f32[1152]{0:T(1024)S(1)}, f32[1152]{0:T(1024)}, u32[]{:S(2)}) copy-start(f32[1152]{0:T(1024)} %gain_ref.2) | copy-start | bytes 13828
  63.4 25.3 %copy-start.2 = (bf16[269,1152]{1,0:T(8,128)(2,1)S(1)}, bf16[269,1152]{1,0:T(8,128)(2,1)}, u32[]{:S(2)}) copy-start(bf16[269,1152]{1,0:T(8,128)(2,1)} %w_out_ref.3) | copy-start | bytes 1859332
  90.5 14.5 %collective-permute-start.6 = (bf16[2432,128]{1,0:T(8,128)(2,1)S(1)}, bf16[2432,128]{1,0:T(8,128)(2,1)S(1)}, u32[]{:S(2)}, u32[]{:S(2)}) collective-permute-start(bf16[2432,128]{1,0:T(8,128)(2,1)S(1)} %shard_map.113), channel_id=1, source_target_pairs={{0,16},{16,0},{1,17},{17,1},{2,18},{18,2},{3,19},{19,3},{4,20},{20... | collective-permute-start | bytes 1867784 | tf_op jit(solution)/shard_map/ppermute | solution.py:276
  129.5 61.6 %copy-start.5 = (f32[1152]{0:T(1024)S(1)}, f32[1152]{0:T(1024)}, u32[]{:S(2)}) copy-start(f32[1152]{0:T(1024)} %gain_ref.3) | copy-start | bytes 13828
  151.7 40.4 %collective-permute-start.7 = (bf16[2432,128]{1,0:T(8,128)(2,1)S(1)}, bf16[2432,128]{1,0:T(8,128)(2,1)S(1)}, u32[]{:S(2)}, u32[]{:S(2)}) collective-permute-start(bf16[2432,128]{1,0:T(8,128)(2,1)S(1)} %bitcast.19), channel_id=1, source_target_pairs={{0,16},{16,0},{1,17},{17,1},{2,18},{18,2},{3,19},{19,3},{4,20},{20... | collective-permute-start | bytes 1867784 | tf_op jit(solution)/shard_map/ppermute | solution.py:276
  157.4 14.8 %collective-permute-start = (bf16[4,24,1152]{2,1,0:T(8,128)(2,1)S(1)}, bf16[4,24,1152]{2,1,0:T(8,128)(2,1)S(1)}, u32[]{:S(2)}, u32[]{:S(2)}) collective-permute-start(bf16[4,24,1152]{2,1,0:T(8,128)(2,1)S(1)} %get-tuple-element.28), channel_id=1, source_target_pairs={{0,1},{1,2},{2,3},{3,0},{4,5},{5,6},{6,7},{7,4},{8,9},{9,10},{10,1... | collective-permute-start | bytes 663560 | tf_op jit(solution)/shard_map/ppermute | solution.py:276
  160.7 11.5 %collective-permute-start.1 = (bf16[4,24,1152]{2,1,0:T(8,128)(2,1)S(1)}, bf16[4,24,1152]{2,1,0:T(8,128)(2,1)S(1)}, u32[]{:S(2)}, u32[]{:S(2)}) collective-permute-start(bf16[4,24,1152]{2,1,0:T(8,128)(2,1)S(1)} %get-tuple-element.29), channel_id=1, source_target_pairs={{0,2},{1,3},{2,0},{3,1},{4,6},{5,7},{6,4},{7,5},{8,10},{9,11},{10,... | collective-permute-start | bytes 663560 | tf_op jit(solution)/shard_map/ppermute | solution.py:276
  163.0 11.4 %collective-permute-start.2 = (bf16[4,24,1152]{2,1,0:T(8,128)(2,1)S(1)}, bf16[4,24,1152]{2,1,0:T(8,128)(2,1)S(1)}, u32[]{:S(2)}, u32[]{:S(2)}) collective-permute-start(bf16[4,24,1152]{2,1,0:T(8,128)(2,1)S(1)} %get-tuple-element.30), channel_id=1, source_target_pairs={{0,3},{1,0},{2,1},{3,2},{4,7},{5,4},{6,5},{7,6},{8,11},{9,8},{10,9... | collective-permute-start | bytes 663560 | tf_op jit(solution)/shard_map/ppermute | solution.py:276
  174.6 11.9 %collective-permute-start.3 = (bf16[24,1152]{1,0:T(8,128)(2,1)S(1)}, bf16[24,1152]{1,0:T(8,128)(2,1)S(1)}, u32[]{:S(2)}, u32[]{:S(2)}) collective-permute-start(bf16[24,1152]{1,0:T(8,128)(2,1)S(1)} %get-tuple-element.32), channel_id=1, source_target_pairs={{0,4},{4,8},{8,12},{12,0},{1,5},{5,9},{9,13},{13,1},{2,6},{6,10},{... | collective-permute-start | bytes 165896 | tf_op jit(solution)/shard_map/ppermute | solution.py:276
  179.0 8.9 %collective-permute-start.4 = (bf16[24,1152]{1,0:T(8,128)(2,1)S(1)}, bf16[24,1152]{1,0:T(8,128)(2,1)S(1)}, u32[]{:S(2)}, u32[]{:S(2)}) collective-permute-start(bf16[24,1152]{1,0:T(8,128)(2,1)S(1)} %get-tuple-element.33), channel_id=1, source_target_pairs={{0,8},{4,12},{8,0},{12,4},{1,9},{5,13},{9,1},{13,5},{2,10},{6,14},... | collective-permute-start | bytes 165896 | tf_op jit(solution)/shard_map/ppermute | solution.py:276
  181.4 9.7 %collective-permute-start.5 = (bf16[24,1152]{1,0:T(8,128)(2,1)S(1)}, bf16[24,1152]{1,0:T(8,128)(2,1)S(1)}, u32[]{:S(2)}, u32[]{:S(2)}) collective-permute-start(bf16[24,1152]{1,0:T(8,128)(2,1)S(1)} %get-tuple-element.34), channel_id=1, source_target_pairs={{0,12},{4,0},{8,4},{12,8},{1,13},{5,1},{9,5},{13,9},{2,14},{6,2},{... | collective-permute-start | bytes 165896 | tf_op jit(solution)/shard_map/ppermute | solution.py:276
where the time goes:
time: 194 us
  blocking collectives  121 us (62%)
  starting transfers between devices  45.8 us (24%)
  waiting for transfers between devices  13.1 us (7%)
  Pallas kernels  11.6 us (6%)
    ppermute x8, starting transfers between devices, shift(): lax.ppermute(value, axis, [(i, (i + by) % length) for i in range(length)])  39.2 us
    all_to_all x1, blocking collectives, per_device(): group_grads = lax.all_to_all(copies, ARRIVAL, 0, 0)  25.3 us
    all_to_all x1, blocking collectives, per_device(): slices = lax.all_to_all(mine, RING, 0, 0)  24.3 us
    all_to_all x1, blocking collectives, per_device(): whole = lax.all_to_all(copies, RING, 0, 0).reshape(tall, LANES)  22.2 us
    all_gather x1, blocking collectives, per_device(): both = lax.all_gather(own_rows, 'zh')  20.2 us
    all_gather x1, blocking collectives, per_device(): images = lax.all_gather(column, 'x')  17.8 us
    ppermute x8, waiting for transfers between devices, shift(): lax.ppermute(value, axis, [(i, (i + by) % length) for i in range(length)])  13.1 us
    all_gather x1, blocking collectives, per_device(): group_input = lax.all_gather(rows_column, 'x')  11.7 us
  transfers between devices with their start and end apart: 9, of which 5 were waited for; matrix products, arithmetic and copies ran while one was open for 0% of the time, Pallas kernels for 1%

commit v1 on v0

--- a/solution.py
+++ b/solution.py
@@ -230,30 +230,31 @@
         out_ref[k] = sent
 
 
-def unpack(mine_ref, other_ref, w_out_ref, w_in_ref):
-    units, width = w_out_ref.shape
+def unpack(owner, src_ref, *refs):
+    w_out_hbm, w_in_hbm, full_ref, sem = refs[-4:]
+    units, width = full_ref.shape
     core = lax.axis_index("co")
     blocks = width // LANES
     even = units // 8 * 8
     odd = units - even
-
-    def spread(src, dst):
-        for c in range(blocks):
-            lanes = slice(c * LANES, (c + 1) * LANES)
-            dst[:even, lanes] = src[c * even : (c + 1) * even, :].astype(F32)
-            if odd:
-                at = blocks * even + c * odd
-                dst[even:, lanes] = src[at : at + odd, :].astype(F32)
-
-    @pl.when(core == 0)
+    for c in range(blocks):
+        lanes = slice(c * LANES, (c + 1) * LANES)
+        full_ref[:even, lanes] = src_ref[c * even : (c + 1) * even, :].astype(F32)
+        if odd:
+            at = blocks * even + c * odd
+            full_ref[even:, lanes] = src_ref[at : at + odd, :].astype(F32)
+
+    @pl.when(core == owner)
     def _():
-        spread(mine_ref, w_out_ref)
-        spread(other_ref, w_in_ref)
-
-    @pl.when(core != 0)
+        move = pltpu.make_async_copy(full_ref, w_out_hbm, sem)
+        move.start()
+        move.wait()
+
+    @pl.when(core != owner)
     def _():
-        spread(other_ref, w_out_ref)
-        spread(mine_ref, w_in_ref)
+        move = pltpu.make_async_copy(full_ref, w_in_hbm, sem)
+        move.start()
+        move.wait()
 
 
 def column_sum(k0, k1, k2, k3, keep_ref, s1, s2, s3, held):
@@ -274,6 +275,23 @@
 def shift(value, axis, by):
     length = lax.axis_size(axis)
     return lax.ppermute(value, axis, [(i, (i + by) % length) for i in range(length)])
+
+
+def unpack_call(owner, src, whole, units, width):
+    far = pl.BlockSpec(memory_space=pl.ANY)
+    near = pl.BlockSpec(memory_space=pltpu.VMEM)
+    return pl.pallas_call(
+        lambda *refs: unpack(owner, *refs),
+        out_shape=(shape((units, width), F32),) * 2,
+        in_specs=[near] + [far] * len(whole),
+        out_specs=(far, far),
+        scratch_shapes=[pltpu.VMEM((units, width), F32), pltpu.SemaphoreType.DMA(())],
+        input_output_aliases={k + 1: k for k in range(len(whole))},
+        compiler_params=pltpu.CompilerParams(vmem_limit_bytes=VMEM_GRANT),
+        cost_estimate=pl.CostEstimate(
+            flops=0, bytes_accessed=6 * units * width, transcendentals=0
+        ),
+    )(src, *whole)
 
 
 def per_device(
@@ -380,7 +398,8 @@
     (copies,) = call(ring_sum, [shape((ring, chunk, LANES), BF16)], slices)
     whole = lax.all_to_all(copies, RING, 0, 0).reshape(tall, LANES)
     other = shift(whole, "co", 1)
-    grad_w_out, grad_w_in = call(unpack, [shape((units, width), F32)] * 2, whole, other)
+    grad_w_out, grad_w_in = unpack_call(0, whole, (), units, width)
+    grad_w_out, grad_w_in = unpack_call(1, other, (grad_w_out, grad_w_in), units, width)
     return (grad_hidden, grad_w_in.T, grad_w_out)
 
 

time: 194 us -> 195 us (level)
    pallas_call x0 -> x2, Pallas kernels: none -> 2.26 us  [unpack_call(): pl.pallas_call(lambda *refs: unpack(owner, *refs), out_shape=(shape((unit...]
    pallas_call x14 -> x13, Pallas kernels: 11.6 us -> 9.99 us  [call(): pl.pallas_call(body, out_shape=tuple(outs), in_specs=[far if k in far_in...]
  transfers between devices with their start and end apart: 9 -> 9, of which waited for: 5 -> 5; matrix products, arithmetic and copies ran while one was open for 0% -> 0% of each run, Pallas kernels for 1% -> 2%
where the time goes in v1:
time: 195 us; the launch traced here: 194 us
  blocking collectives  121 us (62%)
  starting transfers between devices  45.8 us (23%)
  waiting for transfers between devices  13.1 us (7%)
  Pallas kernels  12.2 us (6%)
    ppermute x8, starting transfers between devices, shift(): lax.ppermute(value, axis, [(i, (i + by) % length) for i in range(length)])  39.2 us
    all_to_all x1, blocking collectives, per_device(): group_grads = lax.all_to_all(copies, ARRIVAL, 0, 0)  25.3 us
    all_to_all x1, blocking collectives, per_device(): slices = lax.all_to_all(mine, RING, 0, 0)  24.3 us
    all_to_all x1, blocking collectives, per_device(): whole = lax.all_to_all(copies, RING, 0, 0).reshape(tall, LANES)  22.2 us
    all_gather x1, blocking collectives, per_device(): both = lax.all_gather(own_rows, 'zh')  20.2 us
    all_gather x1, blocking collectives, per_device(): images = lax.all_gather(column, 'x')  17.8 us
    ppermute x8, waiting for transfers between devices, shift(): lax.ppermute(value, axis, [(i, (i + by) % length) for i in range(length)])  13.1 us
    all_gather x1, blocking collectives, per_device(): group_input = lax.all_gather(rows_column, 'x')  11.7 us
  transfers between devices with their start and end apart: 9, of which 5 were waited for; matrix products, arithmetic and copies ran while one was open for 0% of the time, Pallas kernels for 2%

profile of v1, /device:TPU:1, one launch (start us, length us, event | category | flops | bytes accessed | tf_op | source)
XLA Modules:
  0.0 194.3 jit_solution(1028059983988065602)
XLA Ops:
  0.7 1.8 shard_map.103
  2.5 20.2 %all-gather = bf16[96,2432]{1,0:T(8,128)(2,1)S(1)} all-gather(bf16[24,2432]{1,0:T(8,128)(2,1)} %shard_map.103), channel_id=2, replica_groups=mesh['zl'=2,'y'=8,'co'=2,'zh'=4,'x'=4] {'zh'}, dimensions={0}, use_global_device_ids=true | all-gather | bytes 583680 | tf_op jit(solution)/shard_map/all_gather | solution.py:328
  22.7 0.7 copy-done.4
  23.4 11.7 %all-gather.1 = bf16[16,24,1152]{2,1,0:T(8,128)(2,1)S(1)} all-gather(bf16[4,24,1152]{2,1,0:T(8,128)(2,1)S(1)} %get-tuple-element.23), channel_id=3, replica_groups=mesh['zl'=2,'y'=8,'co'=2,'zh'=4,'x'=4] {'x'}, dimensions={0}, use_global_device_ids=true | all-gather | bytes 1105920 | tf_op jit(solution)/shard_map/all_gather | solution.py:332
  35.2 2.2 %shard_map.105 = bf16[16,24,1152]{2,1,0:T(8,128)(2,1)} custom-call(bf16[4,4,24,1152]{3,2,1,0:T(8,128)(2,1)S(1)} %bitcast.10, bf16[269,1152]{1,0:T(8,128)(2,1)S(1)} %bitcast.16, bf16[269,1152]{1,0:T(8,128)(2,1)S(1)} %copy-done.1), custom_call_target="tpu_custom_call" | custom-call | flops 475987968 | bytes 3009024 | tf_op jit(solution)/shard_map/pallas_call | solution.py:39
  37.4 6.6 %all-to-all-start = ((bf16[16,24,1152]{2,1,0:T(8,128)(2,1)}), bf16[16,24,1152]{2,1,0:T(8,128)(2,1)S(1)}, u32[]{:S(2)}, u32[]{:S(2)}) async-start(bf16[16,24,1152]{2,1,0:T(8,128)(2,1)} %shard_map.105), calls=%async_computation | async-start | bytes 1769472 | tf_op jit(solution)/shard_map/all_to_all | solution.py:337
  44.1 17.8 %all-gather.2 = bf16[16,24,1280]{2,1,0:T(8,128)(2,1)S(1)} all-gather(bf16[4,24,1280]{2,1,0:T(8,128)(2,1)} %copy-done.4), channel_id=4, replica_groups=mesh['zl'=2,'y'=8,'co'=2,'zh'=4,'x'=4] {'x'}, dimensions={0}, use_global_device_ids=true | all-gather | bytes 1228800 | tf_op jit(solution)/shard_map/all_gather | solution.py:335
  61.9 0.2 shard_map.106.target_ref
  62.1 1.3 shard_map.107
  63.4 25.3 %all_to_all.20.rows_ref.refs_1_ = bf16[16,24,1152]{2,1,0:T(8,128)(2,1)S(1)} all-to-all(bf16[16,24,1152]{2,1,0:T(8,128)(2,1)S(1)} %get-tuple-element.27), channel_id=1, replica_groups=mesh['zl'=2,'y'=8,'co'=2,'zh'=4,'x'=4] {'x','zh'}, dimensions={0} | all-to-all | bytes 1769472 | tf_op jit(solution)/shard_map/all_to_all | solution.py:341
  88.7 1.2 shard_map.108
  89.9 0.6 shard_map.113
  90.5 12.8 %collective-permute-start.6 = (bf16[2432,128]{1,0:T(8,128)(2,1)S(1)}, bf16[2432,128]{1,0:T(8,128)(2,1)S(1)}, u32[]{:S(2)}, u32[]{:S(2)}) collective-permute-start(bf16[2432,128]{1,0:T(8,128)(2,1)S(1)} %shard_map.113), channel_id=1, source_target_pairs={{0,16},{16,0},{1,17},{17,1},{2,18},{18,2},{3,19},{19,3},{4,20},{20... | collective-permute-start | bytes 1867784 | tf_op jit(solution)/shard_map/ppermute | solution.py:277
  103.3 0.6 shard_map.112.kept_ref
  103.9 1.1 collective-permute-done.6.got_ref
  105.1 24.3 %all_to_all.21.slices_ref = bf16[16,152,128]{2,1,0:T(8,128)(2,1)S(1)} all-to-all(bf16[16,152,128]{2,1,0:T(8,128)(2,1)S(1)} %shard_map.114), channel_id=1, replica_groups=mesh['zl'=2,'y'=8,'co'=2,'zh'=4,'x'=4] {'zl','y'}, dimensions={0} | all-to-all | bytes 1245184 | tf_op jit(solution)/shard_map/all_to_all | solution.py:370
  129.5 22.2 %all_to_all.22 = bf16[16,152,128]{2,1,0:T(8,128)(2,1)S(1)} all-to-all(bf16[16,152,128]{2,1,0:T(8,128)(2,1)S(1)} %shard_map.115), channel_id=1, replica_groups=mesh['zl'=2,'y'=8,'co'=2,'zh'=4,'x'=4] {'zl','y'}, dimensions={0} | all-to-all | bytes 1245184 | tf_op jit(solution)/shard_map/all_to_all | solution.py:399
  151.7 5.0 %collective-permute-start.7 = (bf16[2432,128]{1,0:T(8,128)(2,1)S(1)}, bf16[2432,128]{1,0:T(8,128)(2,1)S(1)}, u32[]{:S(2)}, u32[]{:S(2)}) collective-permute-start(bf16[2432,128]{1,0:T(8,128)(2,1)S(1)} %bitcast.19), channel_id=1, source_target_pairs={{0,16},{16,0},{1,17},{17,1},{2,18},{18,2},{3,19},{19,3},{4,20},{20... | collective-permute-start | bytes 1867784 | tf_op jit(solution)/shard_map/ppermute | solution.py:277
  156.6 0.7 shard_map.109
  157.4 3.3 %collective-permute-start = (bf16[4,24,1152]{2,1,0:T(8,128)(2,1)S(1)}, bf16[4,24,1152]{2,1,0:T(8,128)(2,1)S(1)}, u32[]{:S(2)}, u32[]{:S(2)}) collective-permute-start(bf16[4,24,1152]{2,1,0:T(8,128)(2,1)S(1)} %get-tuple-element.30), channel_id=1, source_target_pairs={{0,1},{1,2},{2,3},{3,0},{4,5},{5,6},{6,7},{7,4},{8,9},{9,10},{10,1... | collective-permute-start | bytes 663560 | tf_op jit(solution)/shard_map/ppermute | solution.py:277
  160.7 2.3 %collective-permute-start.1 = (bf16[4,24,1152]{2,1,0:T(8,128)(2,1)S(1)}, bf16[4,24,1152]{2,1,0:T(8,128)(2,1)S(1)}, u32[]{:S(2)}, u32[]{:S(2)}) collective-permute-start(bf16[4,24,1152]{2,1,0:T(8,128)(2,1)S(1)} %get-tuple-element.31), channel_id=1, source_target_pairs={{0,2},{1,3},{2,0},{3,1},{4,6},{5,7},{6,4},{7,5},{8,10},{9,11},{10,... | collective-permute-start | bytes 663560 | tf_op jit(solution)/shard_map/ppermute | solution.py:277
  163.0 4.0 %collective-permute-start.2 = (bf16[4,24,1152]{2,1,0:T(8,128)(2,1)S(1)}, bf16[4,24,1152]{2,1,0:T(8,128)(2,1)S(1)}, u32[]{:S(2)}, u32[]{:S(2)}) collective-permute-start(bf16[4,24,1152]{2,1,0:T(8,128)(2,1)S(1)} %get-tuple-element.32), channel_id=1, source_target_pairs={{0,3},{1,0},{2,1},{3,2},{4,7},{5,4},{6,5},{7,6},{8,11},{9,8},{10,9... | collective-permute-start | bytes 663560 | tf_op jit(solution)/shard_map/ppermute | solution.py:277
  166.9 5.2 %collective-permute-done.k1 = bf16[4,24,1152]{2,1,0:T(8,128)(2,1)S(1)} collective-permute-done((bf16[4,24,1152]{2,1,0:T(8,128)(2,1)S(1)}, bf16[4,24,1152]{2,1,0:T(8,128)(2,1)S(1)}, u32[]{:S(2)}, u32[]{:S(2)}) %collective-permute-start) | collective-permute-done | bytes 221216 | tf_op jit(solution)/shard_map/ppermute | solution.py:277
  172.2 2.2 %collective-permute-done.2.k3 = bf16[4,24,1152]{2,1,0:T(8,128)(2,1)S(1)} collective-permute-done((bf16[4,24,1152]{2,1,0:T(8,128)(2,1)S(1)}, bf16[4,24,1152]{2,1,0:T(8,128)(2,1)S(1)}, u32[]{:S(2)}, u32[]{:S(2)}) %collective-permute-start.2) | collective-permute-done | bytes 221216 | tf_op jit(solution)/shard_map/ppermute | solution.py:277
  174.6 4.4 %collective-permute-start.3 = (bf16[24,1152]{1,0:T(8,128)(2,1)S(1)}, bf16[24,1152]{1,0:T(8,128)(2,1)S(1)}, u32[]{:S(2)}, u32[]{:S(2)}) collective-permute-start(bf16[24,1152]{1,0:T(8,128)(2,1)S(1)} %get-tuple-element.34), channel_id=1, source_target_pairs={{0,4},{4,8},{8,12},{12,0},{1,5},{5,9},{9,13},{13,1},{2,6},{6,10},{... | collective-permute-start | bytes 165896 | tf_op jit(solution)/shard_map/ppermute | solution.py:277
  179.0 2.4 %collective-permute-start.4 = (bf16[24,1152]{1,0:T(8,128)(2,1)S(1)}, bf16[24,1152]{1,0:T(8,128)(2,1)S(1)}, u32[]{:S(2)}, u32[]{:S(2)}) collective-permute-start(bf16[24,1152]{1,0:T(8,128)(2,1)S(1)} %get-tuple-element.35), channel_id=1, source_target_pairs={{0,8},{4,12},{8,0},{12,4},{1,9},{5,13},{9,1},{13,5},{2,10},{6,14},... | collective-permute-start | bytes 165896 | tf_op jit(solution)/shard_map/ppermute | solution.py:277
  181.4 5.0 %collective-permute-start.5 = (bf16[24,1152]{1,0:T(8,128)(2,1)S(1)}, bf16[24,1152]{1,0:T(8,128)(2,1)S(1)}, u32[]{:S(2)}, u32[]{:S(2)}) collective-permute-start(bf16[24,1152]{1,0:T(8,128)(2,1)S(1)} %get-tuple-element.36), channel_id=1, source_target_pairs={{0,12},{4,0},{8,4},{12,8},{1,13},{5,1},{9,5},{13,9},{2,14},{6,2},{... | collective-permute-start | bytes 165896 | tf_op jit(solution)/shard_map/ppermute | solution.py:277
  186.5 1.3 collective-permute-done.4.g2
  187.8 3.2 %collective-permute-done.5.g3 = bf16[24,1152]{1,0:T(8,128)(2,1)S(1)} collective-permute-done((bf16[24,1152]{1,0:T(8,128)(2,1)S(1)}, bf16[24,1152]{1,0:T(8,128)(2,1)S(1)}, u32[]{:S(2)}, u32[]{:S(2)}) %collective-permute-start.5) | collective-permute-done | bytes 55328 | tf_op jit(solution)/shard_map/ppermute | solution.py:277
  191.1 0.9 shard_map.111
  192.0 1.1 shard_map.116
  193.2 1.1 shard_map.117
  (25 shorter events, 0.5 us)
Async XLA Ops:
  0.6 34.5 %copy-start.1 = (bf16[269,1152]{1,0:T(8,128)(2,1)S(1)}, bf16[269,1152]{1,0:T(8,128)(2,1)}, u32[]{:S(2)}) copy-start(bf16[269,1152]{1,0:T(8,128)(2,1)} %w_out_ref.3) | copy-start | bytes 1859332
  0.6 34.5 %copy-start = (bf16[1152,269]{0,1:T(8,128)(2,1)S(1)}, bf16[1152,269]{0,1:T(8,128)(2,1)}, u32[]{:S(2)}) copy-start(bf16[1152,269]{0,1:T(8,128)(2,1)} %param.11) | copy-start | bytes 1859332
  22.7 0.7 copy-start.4
  37.4 24.5 %copy-start.6 = (bf16[1,384,24]{1,2,0:T(8,128)(2,1)S(1)}, bf16[1,384,24]{1,2,0:T(8,128)(2,1)}, u32[]{:S(2)}) copy-start(bf16[1,384,24]{1,2,0:T(8,128)(2,1)} %param.15) | copy-start | bytes 55300
  37.4 24.5 %copy-start.8 = (s32[24]{0:T(128)S(1)}, s32[24]{0:T(128)}, u32[]{:S(2)}) copy-start(s32[24]{0:T(128)} %param.14) | copy-start | bytes 292
  37.4 24.7 %all-to-all-start = ((bf16[16,24,1152]{2,1,0:T(8,128)(2,1)}), bf16[16,24,1152]{2,1,0:T(8,128)(2,1)S(1)}, u32[]{:S(2)}, u32[]{:S(2)}) async-start(bf16[16,24,1152]{2,1,0:T(8,128)(2,1)} %shard_map.105), calls=%async_computation | async-start | bytes 1769472 | tf_op jit(solution)/shard_map/all_to_all | solution.py:337
  44.1 18.1 %copy-start.3 = (bf16[24,1152]{1,0:T(8,128)(2,1)S(1)}, bf16[24,1152]{1,0:T(8,128)(2,1)}, u32[]{:S(2)}) copy-start(bf16[24,1152]{1,0:T(8,128)(2,1)} %hidden_ref.3) | copy-start | bytes 165892
  44.1 18.1 %copy-start.7 = (f32[1152]{0:T(1024)S(1)}, f32[1152]{0:T(1024)}, u32[]{:S(2)}) copy-start(f32[1152]{0:T(1024)} %gain_ref.2) | copy-start | bytes 13828
  63.4 25.3 %copy-start.2 = (bf16[269,1152]{1,0:T(8,128)(2,1)S(1)}, bf16[269,1152]{1,0:T(8,128)(2,1)}, u32[]{:S(2)}) copy-start(bf16[269,1152]{1,0:T(8,128)(2,1)} %w_out_ref.3) | copy-start | bytes 1859332
  90.5 14.5 %collective-permute-start.6 = (bf16[2432,128]{1,0:T(8,128)(2,1)S(1)}, bf16[2432,128]{1,0:T(8,128)(2,1)S(1)}, u32[]{:S(2)}, u32[]{:S(2)}) collective-permute-start(bf16[2432,128]{1,0:T(8,128)(2,1)S(1)} %shard_map.113), channel_id=1, source_target_pairs={{0,16},{16,0},{1,17},{17,1},{2,18},{18,2},{3,19},{19,3},{4,20},{20... | collective-permute-start | bytes 1867784 | tf_op jit(solution)/shard_map/ppermute | solution.py:277
  129.5 61.6 %copy-start.5 = (f32[1152]{0:T(1024)S(1)}, f32[1152]{0:T(1024)}, u32[]{:S(2)}) copy-start(f32[1152]{0:T(1024)} %gain_ref.3) | copy-start | bytes 13828
  151.7 41.5 %collective-permute-start.7 = (bf16[2432,128]{1,0:T(8,128)(2,1)S(1)}, bf16[2432,128]{1,0:T(8,128)(2,1)S(1)}, u32[]{:S(2)}, u32[]{:S(2)}) collective-permute-start(bf16[2432,128]{1,0:T(8,128)(2,1)S(1)} %bitcast.19), channel_id=1, source_target_pairs={{0,16},{16,0},{1,17},{17,1},{2,18},{18,2},{3,19},{19,3},{4,20},{20... | collective-permute-start | bytes 1867784 | tf_op jit(solution)/shard_map/ppermute | solution.py:277
  157.4 14.8 %collective-permute-start = (bf16[4,24,1152]{2,1,0:T(8,128)(2,1)S(1)}, bf16[4,24,1152]{2,1,0:T(8,128)(2,1)S(1)}, u32[]{:S(2)}, u32[]{:S(2)}) collective-permute-start(bf16[4,24,1152]{2,1,0:T(8,128)(2,1)S(1)} %get-tuple-element.30), channel_id=1, source_target_pairs={{0,1},{1,2},{2,3},{3,0},{4,5},{5,6},{6,7},{7,4},{8,9},{9,10},{10,1... | collective-permute-start | bytes 663560 | tf_op jit(solution)/shard_map/ppermute | solution.py:277
  160.7 11.5 %collective-permute-start.1 = (bf16[4,24,1152]{2,1,0:T(8,128)(2,1)S(1)}, bf16[4,24,1152]{2,1,0:T(8,128)(2,1)S(1)}, u32[]{:S(2)}, u32[]{:S(2)}) collective-permute-start(bf16[4,24,1152]{2,1,0:T(8,128)(2,1)S(1)} %get-tuple-element.31), channel_id=1, source_target_pairs={{0,2},{1,3},{2,0},{3,1},{4,6},{5,7},{6,4},{7,5},{8,10},{9,11},{10,... | collective-permute-start | bytes 663560 | tf_op jit(solution)/shard_map/ppermute | solution.py:277
  163.0 11.4 %collective-permute-start.2 = (bf16[4,24,1152]{2,1,0:T(8,128)(2,1)S(1)}, bf16[4,24,1152]{2,1,0:T(8,128)(2,1)S(1)}, u32[]{:S(2)}, u32[]{:S(2)}) collective-permute-start(bf16[4,24,1152]{2,1,0:T(8,128)(2,1)S(1)} %get-tuple-element.32), channel_id=1, source_target_pairs={{0,3},{1,0},{2,1},{3,2},{4,7},{5,4},{6,5},{7,6},{8,11},{9,8},{10,9... | collective-permute-start | bytes 663560 | tf_op jit(solution)/shard_map/ppermute | solution.py:277
  174.6 11.9 %collective-permute-start.3 = (bf16[24,1152]{1,0:T(8,128)(2,1)S(1)}, bf16[24,1152]{1,0:T(8,128)(2,1)S(1)}, u32[]{:S(2)}, u32[]{:S(2)}) collective-permute-start(bf16[24,1152]{1,0:T(8,128)(2,1)S(1)} %get-tuple-element.34), channel_id=1, source_target_pairs={{0,4},{4,8},{8,12},{12,0},{1,5},{5,9},{9,13},{13,1},{2,6},{6,10},{... | collective-permute-start | bytes 165896 | tf_op jit(solution)/shard_map/ppermute | solution.py:277
  179.0 8.9 %collective-permute-start.4 = (bf16[24,1152]{1,0:T(8,128)(2,1)S(1)}, bf16[24,1152]{1,0:T(8,128)(2,1)S(1)}, u32[]{:S(2)}, u32[]{:S(2)}) collective-permute-start(bf16[24,1152]{1,0:T(8,128)(2,1)S(1)} %get-tuple-element.35), channel_id=1, source_target_pairs={{0,8},{4,12},{8,0},{12,4},{1,9},{5,13},{9,1},{13,5},{2,10},{6,14},... | collective-permute-start | bytes 165896 | tf_op jit(solution)/shard_map/ppermute | solution.py:277
  181.4 9.7 %collective-permute-start.5 = (bf16[24,1152]{1,0:T(8,128)(2,1)S(1)}, bf16[24,1152]{1,0:T(8,128)(2,1)S(1)}, u32[]{:S(2)}, u32[]{:S(2)}) collective-permute-start(bf16[24,1152]{1,0:T(8,128)(2,1)S(1)} %get-tuple-element.36), channel_id=1, source_target_pairs={{0,12},{4,0},{8,4},{12,8},{1,13},{5,1},{9,5},{13,9},{2,14},{6,2},{... | collective-permute-start | bytes 165896 | tf_op jit(solution)/shard_map/ppermute | solution.py:277

commit v2 on v1

--- a/solution.py
+++ b/solution.py
@@ -91,10 +91,12 @@
     moves = [pltpu.make_async_copy(src, dst, sems.at[k]) for k, (src, dst) in enumerate(arrays)]
     for move in moves:
         move.start()
-    for move in moves:
-        move.wait()
+    moves[0].wait()
     normed, _ = norm_parts(hidden_ref[...].astype(F32))
+    moves[1].wait()
     out_ref[:, :width] = (normed * gain_ref[...].reshape(1, width)).astype(BF16)
+    moves[2].wait()
+    moves[3].wait()
     image = image_ref[...].astype(F32)
     scale = lax.rsqrt(jnp.sum(image * image, axis=-1, keepdims=True) + epsilon)
     out_ref[:, width : 2 * width] = (image * scale).astype(BF16)
@@ -163,7 +165,7 @@
         out_ref[k] = sent
 
 
-def backward(all_ref, w_in_ref, rows_ref, w_out_ref, grad_ref, act_ref):
+def backward(all_ref, w_in_ref, rows_ref, w_out_ref, grad_ref, act_ref, give_ref):
     blocks, rows, width = rows_ref.shape
     group = blocks * rows
     pre_act = dot(all_ref[...].reshape(group, width), w_in_ref[...], NT)
@@ -171,6 +173,7 @@
     act_ref[...] = value.astype(BF16)
     grad_act = dot(rows_ref[...].reshape(group, width), w_out_ref[...], NT)
     grad_ref[...] = (grad_act * slope).astype(BF16)
+    weight_grad(1, act_ref, rows_ref, grad_ref, all_ref, give_ref)
 
 
 def input_grad(grad_ref, w_in_ref, k0, k1, k2, k3, held):
@@ -339,18 +342,18 @@
         middle, [spread, shape((rows, width), F32)], parts, hidden_in, gain_final, images, target
     )
     group_grads = lax.all_to_all(copies, ARRIVAL, 0, 0)
-    grad_pre, act = call(
+    chunk = -(-(units * (width // LANES)) // (8 * ring)) * 8
+    tall = chunk * ring
+
+    grad_pre, act, give = call(
         backward,
-        [shape((group, units), BF16)] * 2,
+        [shape((group, units), BF16)] * 2 + [shape((tall, LANES), BF16)],
         group_input,
         w_in_rows,
         group_grads,
         w_out,
-        flops=2 * matmul,
-    )
-
-    chunk = -(-(units * (width // LANES)) // (8 * ring)) * 8
-    tall = chunk * ring
+        flops=3 * matmul,
+    )
 
     def grads(first, dtype):
         return call(
@@ -363,7 +366,6 @@
             flops=matmul,
         )[0]
 
-    give = grads(1, BF16)
     got = shift(give, "co", 1)
     keep = grads(0, F32)
     (mine,) = call(join, [shape((ring, chunk, LANES), BF16)], keep, got)

time: 195 us -> 195 us (level)
    pallas_call x13 -> x12, Pallas kernels: 9.99 us -> 10 us  [call(): pl.pallas_call(body, out_shape=tuple(outs), in_specs=[far if k in far_in...]
where the time goes in v2:
time: 195 us; the launch traced here: 194 us
  blocking collectives  121 us (62%)
  starting transfers between devices  45.9 us (24%)
  waiting for transfers between devices  13.2 us (7%)
  Pallas kernels  12.3 us (6%)
    ppermute x8, starting transfers between devices, shift(): lax.ppermute(value, axis, [(i, (i + by) % length) for i in range(length)])  39.2 us
    all_to_all x1, blocking collectives, per_device(): group_grads = lax.all_to_all(copies, ARRIVAL, 0, 0)  25.2 us
    all_to_all x1, blocking collectives, per_device(): slices = lax.all_to_all(mine, RING, 0, 0)  24.4 us
    all_to_all x1, blocking collectives, per_device(): whole = lax.all_to_all(copies, RING, 0, 0).reshape(tall, LANES)  22.2 us
    all_gather x1, blocking collectives, per_device(): both = lax.all_gather(own_rows, 'zh')  20.2 us
    all_gather x1, blocking collectives, per_device(): images = lax.all_gather(column, 'x')  17.8 us
    ppermute x8, waiting for transfers between devices, shift(): lax.ppermute(value, axis, [(i, (i + by) % length) for i in range(length)])  13.2 us
    all_gather x1, blocking collectives, per_device(): group_input = lax.all_gather(rows_column, 'x')  11.7 us
  transfers between devices with their start and end apart: 9, of which 5 were waited for; matrix products, arithmetic and copies ran while one was open for 0% of the time, Pallas kernels for 2%

profile of v2, /device:TPU:1, one launch (start us, length us, event | category | flops | bytes accessed | tf_op | source)
XLA Modules:
  0.0 194.3 jit_solution(3743140676279159694)
XLA Ops:
  0.7 1.9 shard_map.103
  2.6 20.2 %all-gather = bf16[96,2432]{1,0:T(8,128)(2,1)S(1)} all-gather(bf16[24,2432]{1,0:T(8,128)(2,1)} %shard_map.103), channel_id=2, replica_groups=mesh['zl'=2,'y'=8,'co'=2,'zh'=4,'x'=4] {'zh'}, dimensions={0}, use_global_device_ids=true | all-gather | bytes 583680 | tf_op jit(solution)/shard_map/all_gather | solution.py:331
  22.8 0.7 copy-done.4
  23.5 11.7 %all-gather.1 = bf16[16,24,1152]{2,1,0:T(8,128)(2,1)S(1)} all-gather(bf16[4,24,1152]{2,1,0:T(8,128)(2,1)S(1)} %get-tuple-element.24), channel_id=3, replica_groups=mesh['zl'=2,'y'=8,'co'=2,'zh'=4,'x'=4] {'x'}, dimensions={0}, use_global_device_ids=true | all-gather | bytes 1105920 | tf_op jit(solution)/shard_map/all_gather | solution.py:335
  35.2 2.2 %shard_map.105 = bf16[16,24,1152]{2,1,0:T(8,128)(2,1)} custom-call(bf16[4,4,24,1152]{3,2,1,0:T(8,128)(2,1)S(1)} %bitcast.10, bf16[269,1152]{1,0:T(8,128)(2,1)S(1)} %bitcast.15, bf16[269,1152]{1,0:T(8,128)(2,1)S(1)} %copy-done.1), custom_call_target="tpu_custom_call" | custom-call | flops 475987968 | bytes 3009024 | tf_op jit(solution)/shard_map/pallas_call | solution.py:39
  37.5 6.7 %all-to-all-start = ((bf16[16,24,1152]{2,1,0:T(8,128)(2,1)}), bf16[16,24,1152]{2,1,0:T(8,128)(2,1)S(1)}, u32[]{:S(2)}, u32[]{:S(2)}) async-start(bf16[16,24,1152]{2,1,0:T(8,128)(2,1)} %shard_map.105), calls=%async_computation | async-start | bytes 1769472 | tf_op jit(solution)/shard_map/all_to_all | solution.py:340
  44.1 17.8 %all-gather.2 = bf16[16,24,1280]{2,1,0:T(8,128)(2,1)S(1)} all-gather(bf16[4,24,1280]{2,1,0:T(8,128)(2,1)} %copy-done.4), channel_id=4, replica_groups=mesh['zl'=2,'y'=8,'co'=2,'zh'=4,'x'=4] {'x'}, dimensions={0}, use_global_device_ids=true | all-gather | bytes 1228800 | tf_op jit(solution)/shard_map/all_gather | solution.py:338
  61.9 0.2 shard_map.106.target_ref
  62.2 1.3 shard_map.107
  63.5 25.2 %all_to_all.20.rows_ref.refs_1_ = bf16[16,24,1152]{2,1,0:T(8,128)(2,1)S(1)} all-to-all(bf16[16,24,1152]{2,1,0:T(8,128)(2,1)S(1)} %get-tuple-element.28), channel_id=1, replica_groups=mesh['zl'=2,'y'=8,'co'=2,'zh'=4,'x'=4] {'x','zh'}, dimensions={0} | all-to-all | bytes 1769472 | tf_op jit(solution)/shard_map/all_to_all | solution.py:344
  88.7 1.7 shard_map.108
  90.5 12.8 %collective-permute-start.6 = (bf16[2432,128]{1,0:T(8,128)(2,1)S(1)}, bf16[2432,128]{1,0:T(8,128)(2,1)S(1)}, u32[]{:S(2)}, u32[]{:S(2)}) collective-permute-start(bf16[2432,128]{1,0:T(8,128)(2,1)S(1)} %get-tuple-element.40), channel_id=1, source_target_pairs={{0,16},{16,0},{1,17},{17,1},{2,18},{18,2},{3,19},{19,3},{4,20},{20... | collective-permute-start | bytes 1867784 | tf_op jit(solution)/shard_map/ppermute | solution.py:280
  103.3 0.6 shard_map.112.kept_ref
  103.9 1.1 collective-permute-done.6.got_ref
  105.1 24.4 %all_to_all.21.slices_ref = bf16[16,152,128]{2,1,0:T(8,128)(2,1)S(1)} all-to-all(bf16[16,152,128]{2,1,0:T(8,128)(2,1)S(1)} %shard_map.113), channel_id=1, replica_groups=mesh['zl'=2,'y'=8,'co'=2,'zh'=4,'x'=4] {'zl','y'}, dimensions={0} | all-to-all | bytes 1245184 | tf_op jit(solution)/shard_map/all_to_all | solution.py:372
  129.5 22.2 %all_to_all.22 = bf16[16,152,128]{2,1,0:T(8,128)(2,1)S(1)} all-to-all(bf16[16,152,128]{2,1,0:T(8,128)(2,1)S(1)} %shard_map.114), channel_id=1, replica_groups=mesh['zl'=2,'y'=8,'co'=2,'zh'=4,'x'=4] {'zl','y'}, dimensions={0} | all-to-all | bytes 1245184 | tf_op jit(solution)/shard_map/all_to_all | solution.py:401
  151.7 5.0 %collective-permute-start.7 = (bf16[2432,128]{1,0:T(8,128)(2,1)S(1)}, bf16[2432,128]{1,0:T(8,128)(2,1)S(1)}, u32[]{:S(2)}, u32[]{:S(2)}) collective-permute-start(bf16[2432,128]{1,0:T(8,128)(2,1)S(1)} %bitcast.18), channel_id=1, source_target_pairs={{0,16},{16,0},{1,17},{17,1},{2,18},{18,2},{3,19},{19,3},{4,20},{20... | collective-permute-start | bytes 1867784 | tf_op jit(solution)/shard_map/ppermute | solution.py:280
  156.7 0.7 shard_map.109
  157.4 3.3 %collective-permute-start = (bf16[4,24,1152]{2,1,0:T(8,128)(2,1)S(1)}, bf16[4,24,1152]{2,1,0:T(8,128)(2,1)S(1)}, u32[]{:S(2)}, u32[]{:S(2)}) collective-permute-start(bf16[4,24,1152]{2,1,0:T(8,128)(2,1)S(1)} %get-tuple-element.31), channel_id=1, source_target_pairs={{0,1},{1,2},{2,3},{3,0},{4,5},{5,6},{6,7},{7,4},{8,9},{9,10},{10,1... | collective-permute-start | bytes 663560 | tf_op jit(solution)/shard_map/ppermute | solution.py:280
  160.7 2.3 %collective-permute-start.1 = (bf16[4,24,1152]{2,1,0:T(8,128)(2,1)S(1)}, bf16[4,24,1152]{2,1,0:T(8,128)(2,1)S(1)}, u32[]{:S(2)}, u32[]{:S(2)}) collective-permute-start(bf16[4,24,1152]{2,1,0:T(8,128)(2,1)S(1)} %get-tuple-element.32), channel_id=1, source_target_pairs={{0,2},{1,3},{2,0},{3,1},{4,6},{5,7},{6,4},{7,5},{8,10},{9,11},{10,... | collective-permute-start | bytes 663560 | tf_op jit(solution)/shard_map/ppermute | solution.py:280
  163.0 4.0 %collective-permute-start.2 = (bf16[4,24,1152]{2,1,0:T(8,128)(2,1)S(1)}, bf16[4,24,1152]{2,1,0:T(8,128)(2,1)S(1)}, u32[]{:S(2)}, u32[]{:S(2)}) collective-permute-start(bf16[4,24,1152]{2,1,0:T(8,128)(2,1)S(1)} %get-tuple-element.33), channel_id=1, source_target_pairs={{0,3},{1,0},{2,1},{3,2},{4,7},{5,4},{6,5},{7,6},{8,11},{9,8},{10,9... | collective-permute-start | bytes 663560 | tf_op jit(solution)/shard_map/ppermute | solution.py:280
  167.0 5.3 %collective-permute-done.k1 = bf16[4,24,1152]{2,1,0:T(8,128)(2,1)S(1)} collective-permute-done((bf16[4,24,1152]{2,1,0:T(8,128)(2,1)S(1)}, bf16[4,24,1152]{2,1,0:T(8,128)(2,1)S(1)}, u32[]{:S(2)}, u32[]{:S(2)}) %collective-permute-start) | collective-permute-done | bytes 221216 | tf_op jit(solution)/shard_map/ppermute | solution.py:280
  172.2 2.2 %collective-permute-done.2.k3 = bf16[4,24,1152]{2,1,0:T(8,128)(2,1)S(1)} collective-permute-done((bf16[4,24,1152]{2,1,0:T(8,128)(2,1)S(1)}, bf16[4,24,1152]{2,1,0:T(8,128)(2,1)S(1)}, u32[]{:S(2)}, u32[]{:S(2)}) %collective-permute-start.2) | collective-permute-done | bytes 221216 | tf_op jit(solution)/shard_map/ppermute | solution.py:280
  174.4 0.2 shard_map.110
  174.6 4.4 %collective-permute-start.3 = (bf16[24,1152]{1,0:T(8,128)(2,1)S(1)}, bf16[24,1152]{1,0:T(8,128)(2,1)S(1)}, u32[]{:S(2)}, u32[]{:S(2)}) collective-permute-start(bf16[24,1152]{1,0:T(8,128)(2,1)S(1)} %get-tuple-element.35), channel_id=1, source_target_pairs={{0,4},{4,8},{8,12},{12,0},{1,5},{5,9},{9,13},{13,1},{2,6},{6,10},{... | collective-permute-start | bytes 165896 | tf_op jit(solution)/shard_map/ppermute | solution.py:280
  179.0 2.4 %collective-permute-start.4 = (bf16[24,1152]{1,0:T(8,128)(2,1)S(1)}, bf16[24,1152]{1,0:T(8,128)(2,1)S(1)}, u32[]{:S(2)}, u32[]{:S(2)}) collective-permute-start(bf16[24,1152]{1,0:T(8,128)(2,1)S(1)} %get-tuple-element.36), channel_id=1, source_target_pairs={{0,8},{4,12},{8,0},{12,4},{1,9},{5,13},{9,1},{13,5},{2,10},{6,14},... | collective-permute-start | bytes 165896 | tf_op jit(solution)/shard_map/ppermute | solution.py:280
  181.5 5.0 %collective-permute-start.5 = (bf16[24,1152]{1,0:T(8,128)(2,1)S(1)}, bf16[24,1152]{1,0:T(8,128)(2,1)S(1)}, u32[]{:S(2)}, u32[]{:S(2)}) collective-permute-start(bf16[24,1152]{1,0:T(8,128)(2,1)S(1)} %get-tuple-element.37), channel_id=1, source_target_pairs={{0,12},{4,0},{8,4},{12,8},{1,13},{5,1},{9,5},{13,9},{2,14},{6,2},{... | collective-permute-start | bytes 165896 | tf_op jit(solution)/shard_map/ppermute | solution.py:280
  186.5 1.3 collective-permute-done.4.g2
  187.9 3.3 %collective-permute-done.5.g3 = bf16[24,1152]{1,0:T(8,128)(2,1)S(1)} collective-permute-done((bf16[24,1152]{1,0:T(8,128)(2,1)S(1)}, bf16[24,1152]{1,0:T(8,128)(2,1)S(1)}, u32[]{:S(2)}, u32[]{:S(2)}) %collective-permute-start.5) | collective-permute-done | bytes 55328 | tf_op jit(solution)/shard_map/ppermute | solution.py:280
  191.1 0.9 shard_map.111
  192.1 1.1 shard_map.115
  193.2 1.1 shard_map.116
  (24 shorter events, 0.3 us)
Async XLA Ops:
  0.6 34.6 %copy-start.1 = (bf16[269,1152]{1,0:T(8,128)(2,1)S(1)}, bf16[269,1152]{1,0:T(8,128)(2,1)}, u32[]{:S(2)}) copy-start(bf16[269,1152]{1,0:T(8,128)(2,1)} %w_out_ref.3) | copy-start | bytes 1859332
  0.6 34.6 %copy-start = (bf16[1152,269]{0,1:T(8,128)(2,1)S(1)}, bf16[1152,269]{0,1:T(8,128)(2,1)}, u32[]{:S(2)}) copy-start(bf16[1152,269]{0,1:T(8,128)(2,1)} %param.11) | copy-start | bytes 1859332
  22.8 0.7 copy-start.4
  37.5 24.5 %copy-start.6 = (bf16[1,384,24]{1,2,0:T(8,128)(2,1)S(1)}, bf16[1,384,24]{1,2,0:T(8,128)(2,1)}, u32[]{:S(2)}) copy-start(bf16[1,384,24]{1,2,0:T(8,128)(2,1)} %param.15) | copy-start | bytes 55300
  37.5 24.5 %copy-start.8 = (s32[24]{0:T(128)S(1)}, s32[24]{0:T(128)}, u32[]{:S(2)}) copy-start(s32[24]{0:T(128)} %param.14) | copy-start | bytes 292
  37.5 24.7 %all-to-all-start = ((bf16[16,24,1152]{2,1,0:T(8,128)(2,1)}), bf16[16,24,1152]{2,1,0:T(8,128)(2,1)S(1)}, u32[]{:S(2)}, u32[]{:S(2)}) async-start(bf16[16,24,1152]{2,1,0:T(8,128)(2,1)} %shard_map.105), calls=%async_computation | async-start | bytes 1769472 | tf_op jit(solution)/shard_map/all_to_all | solution.py:340
  44.1 18.1 %copy-start.3 = (bf16[24,1152]{1,0:T(8,128)(2,1)S(1)}, bf16[24,1152]{1,0:T(8,128)(2,1)}, u32[]{:S(2)}) copy-start(bf16[24,1152]{1,0:T(8,128)(2,1)} %hidden_ref.3) | copy-start | bytes 165892
  44.1 18.1 %copy-start.7 = (f32[1152]{0:T(1024)S(1)}, f32[1152]{0:T(1024)}, u32[]{:S(2)}) copy-start(f32[1152]{0:T(1024)} %gain_ref.2) | copy-start | bytes 13828
  63.5 25.2 %copy-start.2 = (bf16[269,1152]{1,0:T(8,128)(2,1)S(1)}, bf16[269,1152]{1,0:T(8,128)(2,1)}, u32[]{:S(2)}) copy-start(bf16[269,1152]{1,0:T(8,128)(2,1)} %w_out_ref.3) | copy-start | bytes 1859332
  90.5 14.5 %collective-permute-start.6 = (bf16[2432,128]{1,0:T(8,128)(2,1)S(1)}, bf16[2432,128]{1,0:T(8,128)(2,1)S(1)}, u32[]{:S(2)}, u32[]{:S(2)}) collective-permute-start(bf16[2432,128]{1,0:T(8,128)(2,1)S(1)} %get-tuple-element.40), channel_id=1, source_target_pairs={{0,16},{16,0},{1,17},{17,1},{2,18},{18,2},{3,19},{19,3},{4,20},{20... | collective-permute-start | bytes 1867784 | tf_op jit(solution)/shard_map/ppermute | solution.py:280
  129.5 61.6 %copy-start.5 = (f32[1152]{0:T(1024)S(1)}, f32[1152]{0:T(1024)}, u32[]{:S(2)}) copy-start(f32[1152]{0:T(1024)} %gain_ref.3) | copy-start | bytes 13828
  151.7 41.5 %collective-permute-start.7 = (bf16[2432,128]{1,0:T(8,128)(2,1)S(1)}, bf16[2432,128]{1,0:T(8,128)(2,1)S(1)}, u32[]{:S(2)}, u32[]{:S(2)}) collective-permute-start(bf16[2432,128]{1,0:T(8,128)(2,1)S(1)} %bitcast.18), channel_id=1, source_target_pairs={{0,16},{16,0},{1,17},{17,1},{2,18},{18,2},{3,19},{19,3},{4,20},{20... | collective-permute-start | bytes 1867784 | tf_op jit(solution)/shard_map/ppermute | solution.py:280
  157.4 14.8 %collective-permute-start = (bf16[4,24,1152]{2,1,0:T(8,128)(2,1)S(1)}, bf16[4,24,1152]{2,1,0:T(8,128)(2,1)S(1)}, u32[]{:S(2)}, u32[]{:S(2)}) collective-permute-start(bf16[4,24,1152]{2,1,0:T(8,128)(2,1)S(1)} %get-tuple-element.31), channel_id=1, source_target_pairs={{0,1},{1,2},{2,3},{3,0},{4,5},{5,6},{6,7},{7,4},{8,9},{9,10},{10,1... | collective-permute-start | bytes 663560 | tf_op jit(solution)/shard_map/ppermute | solution.py:280
  160.7 11.5 %collective-permute-start.1 = (bf16[4,24,1152]{2,1,0:T(8,128)(2,1)S(1)}, bf16[4,24,1152]{2,1,0:T(8,128)(2,1)S(1)}, u32[]{:S(2)}, u32[]{:S(2)}) collective-permute-start(bf16[4,24,1152]{2,1,0:T(8,128)(2,1)S(1)} %get-tuple-element.32), channel_id=1, source_target_pairs={{0,2},{1,3},{2,0},{3,1},{4,6},{5,7},{6,4},{7,5},{8,10},{9,11},{10,... | collective-permute-start | bytes 663560 | tf_op jit(solution)/shard_map/ppermute | solution.py:280
  163.0 11.4 %collective-permute-start.2 = (bf16[4,24,1152]{2,1,0:T(8,128)(2,1)S(1)}, bf16[4,24,1152]{2,1,0:T(8,128)(2,1)S(1)}, u32[]{:S(2)}, u32[]{:S(2)}) collective-permute-start(bf16[4,24,1152]{2,1,0:T(8,128)(2,1)S(1)} %get-tuple-element.33), channel_id=1, source_target_pairs={{0,3},{1,0},{2,1},{3,2},{4,7},{5,4},{6,5},{7,6},{8,11},{9,8},{10,9... | collective-permute-start | bytes 663560 | tf_op jit(solution)/shard_map/ppermute | solution.py:280
  174.6 11.9 %collective-permute-start.3 = (bf16[24,1152]{1,0:T(8,128)(2,1)S(1)}, bf16[24,1152]{1,0:T(8,128)(2,1)S(1)}, u32[]{:S(2)}, u32[]{:S(2)}) collective-permute-start(bf16[24,1152]{1,0:T(8,128)(2,1)S(1)} %get-tuple-element.35), channel_id=1, source_target_pairs={{0,4},{4,8},{8,12},{12,0},{1,5},{5,9},{9,13},{13,1},{2,6},{6,10},{... | collective-permute-start | bytes 165896 | tf_op jit(solution)/shard_map/ppermute | solution.py:280
  179.0 8.9 %collective-permute-start.4 = (bf16[24,1152]{1,0:T(8,128)(2,1)S(1)}, bf16[24,1152]{1,0:T(8,128)(2,1)S(1)}, u32[]{:S(2)}, u32[]{:S(2)}) collective-permute-start(bf16[24,1152]{1,0:T(8,128)(2,1)S(1)} %get-tuple-element.36), channel_id=1, source_target_pairs={{0,8},{4,12},{8,0},{12,4},{1,9},{5,13},{9,1},{13,5},{2,10},{6,14},... | collective-permute-start | bytes 165896 | tf_op jit(solution)/shard_map/ppermute | solution.py:280
  181.5 9.7 %collective-permute-start.5 = (bf16[24,1152]{1,0:T(8,128)(2,1)S(1)}, bf16[24,1152]{1,0:T(8,128)(2,1)S(1)}, u32[]{:S(2)}, u32[]{:S(2)}) collective-permute-start(bf16[24,1152]{1,0:T(8,128)(2,1)S(1)} %get-tuple-element.37), channel_id=1, source_target_pairs={{0,12},{4,0},{8,4},{12,8},{1,13},{5,1},{9,5},{13,9},{2,14},{6,2},{... | collective-permute-start | bytes 165896 | tf_op jit(solution)/shard_map/ppermute | solution.py:280
